TPU v7x, 32 devices: a whole 2x2x4 slice. The times are simulated.
32 devices in a mesh: ga: 8 (over z, y), band: 4 (over x, core).
Axes of the slice: x: 2, y: 2, z: 4, core: 2. Of those that a mesh axis runs over, the one named last changes fastest.
Arguments:
- band_coeffs: bfloat16 [8192, 256], P('ga', 'band'), may hold values from -6 to 6
- beta_vectors: bfloat16 [8192, 2048], P('ga'), may hold values from -0.0625 to 0.0625
- atomic_waves: bfloat16 [8192, 1280], P('ga'), may hold values from -0.0625 to 0.0625
- beta_coupling: float32 [2048, 11], replicated, may hold values from -1 to 2
- ortho_inverse: bfloat16 [1280, 1280], replicated, may hold values from -1 to 2
- hubbard_energy: float32 [3], replicated, may hold values from 1 to 4
- band_weight: float32 [256], P('band'), may hold values from 0 to 0.015625
- orbital_start: int32 [1280], replicated, may hold values from 0 to 1277, as said below
- orbital_species: int32 [1280], replicated, may hold values from 0 to 2, as said below
- beta_start: int32 [2048], replicated, may hold values from 0 to 2046, as said below
Outputs:
- hubbard_apply: bfloat16 [8192, 256], P('ga', 'band')
Inputs may be any that keep to these rules, and one draw needn't show every extreme that they name: `orbital_start`: every atom holds 3 or 5 consecutive orbitals; each orbital holds the index of its atom's first orbital. `orbital_species`: orbitals of 5-orbital atoms have species 0 or 1, orbitals of 3-orbital atoms species 2. `beta_start`: every atom holds 2 or 6 consecutive projectors; each projector holds the index of its atom's first projector.
All inputs are finite; a program needn't handle non-finite values.
Results may differ from a plain program's by a relative error of at most 0.0085.
Values sent between devices are 32-bit elements; how exact they have to be, the bound alone decides.
No kernel may reach another device: no remote copies, remote signals or barrier semaphores. Data moves between devices by JAX's collectives and lax.ppermute only.
A program may use at most 64 MiB of HBM per device.

v0:
```python
import jax
import jax.numpy as jnp
from jax import lax
from jax.sharding import PartitionSpec as P

ORB_REACH = 4
BETA_REACH = 5
NSPEC = 3


def rim_shift(extended, reach, offset, rows):
    return lax.slice_in_dim(extended, reach + offset, reach + offset + rows, axis=0)


def same_atom(start_ext, reach, rows):
    centre = rim_shift(start_ext, reach, 0, rows)
    return jnp.stack(
        [
            (rim_shift(start_ext, reach, offset, rows) == centre).astype(jnp.float32)
            for offset in range(-reach, reach + 1)
        ]
    )


def band_apply(coupling, extended, reach, rows):
    total = jnp.zeros((rows, extended.shape[1]), jnp.float32)
    for offset in range(-reach, reach + 1):
        total = total + coupling[offset + reach][:, None] * rim_shift(extended, reach, offset, rows)
    return total


def beta_matrix(beta_coupling, beta_start):
    rows = beta_start.shape[0]
    start_ext = jnp.pad(beta_start, BETA_REACH, constant_values=-1)
    mask = same_atom(start_ext, BETA_REACH, rows)
    padded = jnp.pad(beta_coupling, ((BETA_REACH, BETA_REACH), (0, 0)))
    terms = []
    for offset in range(-BETA_REACH, BETA_REACH + 1):
        mirror = rim_shift(padded, BETA_REACH, offset, rows)[:, BETA_REACH - offset]
        terms.append(0.5 * (beta_coupling[:, BETA_REACH + offset] + mirror))
    return jnp.stack(terms) * mask


def occupancy(extended, weights, mask, reach, rows):
    centre = rim_shift(extended, reach, 0, rows)
    weighted = centre * weights[None, :]
    return (
        jnp.stack(
            [
                jnp.sum(weighted * rim_shift(extended, reach, offset, rows), axis=1)
                for offset in range(-reach, reach + 1)
            ]
        )
        * mask
    )


def hubbard_mix(occupied, u_rows, mask, extended, reach, rows):
    centre_flag = (jnp.arange(2 * reach + 1) == reach).astype(jnp.float32)[:, None]
    potential = u_rows[None, :] * (0.5 * centre_flag - occupied) * mask
    return band_apply(potential, extended, reach, rows)


def per_orbital_u(species, hubbard_energy):
    onehot = (species[:, None] == jnp.arange(NSPEC)[None, :]).astype(jnp.float32)
    return jnp.dot(onehot, hubbard_energy, precision=lax.Precision.HIGHEST)


def shards(
    band_coeffs,
    beta_vectors,
    atomic_waves,
    beta_coupling,
    ortho_inverse,
    hubbard_energy,
    band_weight,
    orbital_start,
    orbital_species,
    beta_start,
):
    highest = lax.Precision.HIGHEST
    nbeta = beta_vectors.shape[1]
    norbit = atomic_waves.shape[1]
    coupling = beta_matrix(beta_coupling, beta_start)
    beta_correlation = lax.psum(
        jnp.dot(beta_vectors.T, band_coeffs, preferred_element_type=jnp.float32), "ga"
    )
    corrected = band_apply(
        coupling, jnp.pad(beta_correlation, ((BETA_REACH, BETA_REACH), (0, 0))), BETA_REACH, nbeta
    ).astype(jnp.bfloat16)
    correlation_psi = (
        band_coeffs.astype(jnp.float32)
        + jnp.dot(beta_vectors, corrected, preferred_element_type=jnp.float32)
    ).astype(jnp.bfloat16)
    partial_value = jnp.dot(atomic_waves.T, correlation_psi, preferred_element_type=jnp.float32)
    u_full = per_orbital_u(orbital_species, hubbard_energy)
    start_full = jnp.pad(orbital_start, ORB_REACH, constant_values=-1)
    ortho_full = ortho_inverse.astype(jnp.float32)
    summed = lax.psum(partial_value, "ga")
    projections = jnp.dot(ortho_full, summed, precision=highest)
    extended = jnp.pad(projections, ((ORB_REACH, ORB_REACH), (0, 0)))
    mask = same_atom(start_full, ORB_REACH, norbit)
    occupied = lax.psum(occupancy(extended, band_weight, mask, ORB_REACH, norbit), "band")
    mixed = hubbard_mix(occupied, u_full, mask, extended, ORB_REACH, norbit)
    rotated = jnp.dot(ortho_full, mixed, precision=highest)
    rotated_half = rotated.astype(jnp.bfloat16)
    hubbard_waves = jnp.dot(atomic_waves, rotated_half, preferred_element_type=jnp.float32)
    wave_half = hubbard_waves.astype(jnp.bfloat16)
    beta_update = lax.psum(
        jnp.dot(beta_vectors.T, wave_half, preferred_element_type=jnp.float32), "ga"
    )
    correction = band_apply(
        coupling, jnp.pad(beta_update, ((BETA_REACH, BETA_REACH), (0, 0))), BETA_REACH, nbeta
    ).astype(jnp.bfloat16)
    return (
        hubbard_waves + jnp.dot(beta_vectors, correction, preferred_element_type=jnp.float32)
    ).astype(jnp.bfloat16)


def solution(mesh):
    placed = (
        P("ga", "band"),
        P("ga", None),
        P("ga", None),
        P(),
        P(),
        P(),
        P("band"),
        P(),
        P(),
        P(),
    )
    return jax.shard_map(
        shards, mesh=mesh, in_specs=placed, out_specs=P("ga", "band"), check_vma=False
    )
```

profile of v0, /device:TPU:0, one launch (start us, length us, event | category | flops | bytes accessed | tf_op | source)
XLA Modules:
  0.0 279.5 jit_solution(14939464274968887758)
XLA Ops:
  6.5 4.1 %fusion.134 = f32[2048,64]{0,1:T(8,128)} fusion(bf16[1024,64]{0,1:T(8,128)(2,1)} %param.10, bf16[1024,2048]{1,0:T(8,128)(2,1)} %param.11), kind=kOutput, calls=%fused_computation.207 | convolution fusion | flops 268435456 | bytes 4849664 | tf_op jit(solution)/shard_map/dot_general | solution.py:86
  10.6 0.0 all-reduce.10.cloned.1.call-update
  10.6 0.0 all-reduce.12.cloned.1.call-start
  10.7 0.1 multiply_bitcast_fusion.8
  10.8 0.9 multiply_bitcast_fusion
  11.6 0.1 fusion.117
  11.7 0.2 stack.181
  11.9 1.7 stack.160
  13.6 0.1 fusion.132
  13.7 72.5 %all-reduce.10.cloned.1.call-done = f32[2048,64]{0,1:T(8,128)} async-done(((f32[2048,64]{0,1:T(8,128)}), f32[2048,64]{0,1:T(8,128)}) %all-reduce.10.cloned.1.call-update) | async-done | bytes 524304 | tf_op jit(solution)/shard_map/psum | solution.py:85
  86.2 8.8 %convolution_bitcast_fusion.2 = f32[1280,64]{0,1:T(8,128)} fusion(bf16[1024,1280]{1,0:T(8,128)(2,1)} %param.12, bf16[1024,2048]{1,0:T(8,128)(2,1)} %param.11, f32[2048,64]{0,1:T(8,128)} %all-reduce.10.cloned.1.call-done, f32[2048]{0:T(1024)S(1)} %bitcast.85, f32[2048]{0:T(1024)S(1)} %bitcast.87, f32[2048]{0:T(1024)S(1)} %bitcast.89, f32[2048]{0:T(1024)S(1)} %bitcast.91, ...), kind=kOutput, calls=%fused_computation.2 | convolution fusion | flops 439287808 | bytes 7888896 | tf_op jit(solution)/shard_map/dot_general | solution.py:95
  95.1 0.0 copy-start.15
  95.1 0.0 all-reduce.12.cloned.1.call-update
  95.1 0.0 all-reduce.14.cloned.1.call-start
  95.2 0.1 fusion.116
  95.4 0.1 stack.208
  95.5 0.5 convolution_reduce_fusion
  96.1 69.8 %all-reduce.12.cloned.1.call-done = f32[1280,64]{0,1:T(8,128)} async-done(((f32[1280,64]{0,1:T(8,128)}), f32[1280,64]{0,1:T(8,128)}) %all-reduce.12.cloned.1.call-update) | async-done | bytes 327696 | tf_op jit(solution)/shard_map/psum | solution.py:99
  165.9 4.0 %convolution_bitcast_fusion.1 = f32[1280,64]{0,1:T(8,128)S(1)} fusion(f32[1280,64]{0,1:T(8,128)} %all-reduce.12.cloned.1.call-done, bf16[1280,1280]{1,0:T(8,128)(2,1)S(1)} %copy-done), kind=kOutput, calls=%fused_computation.1 | convolution fusion | flops 1258291200 | bytes 3932160 | tf_op jit(solution)/shard_map/dot_general | solution.py:100
  169.9 0.7 copy-done.2
  170.6 0.8 fusion.26
  171.5 0.1 stack.191
  171.6 11.1 %psum.30 = f32[9,1280]{1,0:T(8,128)S(1)} all-reduce(f32[9,1280]{1,0:T(8,128)S(1)} %mul.535), channel_id=1, replica_groups=mesh['ga'=8,'band'=4] {'band'}, use_global_device_ids=true, to_apply=%region_11.12 | all-reduce | flops 11520 | bytes 92160 | tf_op jit(solution)/shard_map/psum | solution.py:103
  182.7 0.0 copy-start.1
  182.7 0.1 multiply_multiply_fusion.9
  182.8 0.1 slice_reduce_fusion.8
  183.0 5.8 %convolution_convert_fusion = bf16[64,1280]{1,0:T(8,128)(2,1)S(1)} fusion(bf16[1280,1280]{1,0:T(8,128)(2,1)S(1)} %copy-done, f32[1280,64]{0,1:T(8,128)} %copy-done.2, f32[1280]{0:T(1024)S(1)} %get-tuple-element.15, f32[1280]{0:T(1024)S(1)} %get-tuple-element.16, f32[1280]{0:T(1024)S(1)} %get-tuple-element.17, f32[1280]{0:T(1024)S(1)} %get-tuple-element.18, ...), kind=kOutput, calls=%fused_computation.3 | convolution fusion | flops 1259765760 | bytes 3814400 | tf_op jit(solution)/shard_map/dot_general | solution.py:105
  188.7 2.6 fusion.133
  191.4 1.7 convolution_bitcast_fusion
  193.1 0.0 all-reduce.14.cloned.1.call-update
  193.1 72.4 %all-reduce.14.cloned.1.call-done = f32[2048,64]{0,1:T(8,128)} async-done(((f32[2048,64]{0,1:T(8,128)}), f32[2048,64]{0,1:T(8,128)}) %all-reduce.14.cloned.1.call-update) | async-done | bytes 524304 | tf_op jit(solution)/shard_map/psum | solution.py:109
  265.5 7.5 %fusion.3 = bf16[1024,64]{0,1:T(8,128)(2,1)} fusion(f32[64,1024]{1,0:T(8,128)S(1)} %fusion.133, bf16[1024,2048]{1,0:T(8,128)(2,1)} %param.11, f32[2048,64]{0,1:T(8,128)} %all-reduce.14.cloned.1.call-done, f32[2048]{0:T(1024)S(1)} %bitcast.86, f32[2048]{0:T(1024)} %bitcast.88, f32[2048]{0:T(1024)} %bitcast.90, f32[2048]{0:T(1024)} %bitcast.92, ...), kind=kOutput, calls=%fused_computation.9 | convolution fusion | flops 271450112 | bytes 5201920 | tf_op jit(solution)/shard_map/dot_general | solution.py:116
  (56 shorter events, 0.2 us)
Async XLA Ops:
  6.5 159.3 %copy-start = (bf16[1280,1280]{1,0:T(8,128)(2,1)S(1)}, bf16[1280,1280]{1,0:T(8,128)(2,1)}, u32[]{:S(2)}) copy-start(bf16[1280,1280]{1,0:T(8,128)(2,1)} %param.14) | copy-start | bytes 9830404
  6.5 4.1 %copy-start.3 = (f32[2048,11]{0,1:T(8,128)S(1)}, f32[2048,11]{0,1:T(8,128)}, u32[]{:S(2)}) copy-start(f32[2048,11]{0,1:T(8,128)} %param.13) | copy-start | bytes 270340
  6.5 5.1 %copy-start.14 = (s32[2048]{0:T(1024)S(1)}, s32[2048]{0:T(1024)}, u32[]{:S(2)}) copy-start(s32[2048]{0:T(1024)} %param.19) | copy-start | bytes 24580
  6.5 79.7 %all-reduce.10.cloned.1.call-start = ((), (), s32[]{:S(2)}) async-start(), calls=%async_computation | async-start | bytes 1048576 | tf_op jit(solution)/shard_map/psum | solution.py:85
  10.6 155.2 %all-reduce.12.cloned.1.call-start = ((), (), s32[]{:S(2)}) async-start(), calls=%async_computation.1 | async-start | bytes 655360 | tf_op jit(solution)/shard_map/psum | solution.py:99
  13.7 81.4 %copy-start.5 = (f32[1,2048]{1,0:T(1,128)}, f32[1,2048]{1,0:T(1,128)S(1)}, u32[]{:S(2)}) copy-start(f32[1,2048]{1,0:T(1,128)S(1)} %get-tuple-element.25) | copy-start | bytes 24580
  13.7 81.4 %copy-start.6 = (f32[1,2048]{1,0:T(1,128)}, f32[1,2048]{1,0:T(1,128)S(1)}, u32[]{:S(2)}) copy-start(f32[1,2048]{1,0:T(1,128)S(1)} %get-tuple-element.26) | copy-start | bytes 24580
  13.7 81.3 %copy-start.7 = (f32[1,2048]{1,0:T(1,128)}, f32[1,2048]{1,0:T(1,128)S(1)}, u32[]{:S(2)}) copy-start(f32[1,2048]{1,0:T(1,128)S(1)} %get-tuple-element.27) | copy-start | bytes 24580
  13.7 81.3 %copy-start.8 = (f32[1,2048]{1,0:T(1,128)}, f32[1,2048]{1,0:T(1,128)S(1)}, u32[]{:S(2)}) copy-start(f32[1,2048]{1,0:T(1,128)S(1)} %get-tuple-element.28) | copy-start | bytes 24580
  13.7 81.3 %copy-start.9 = (f32[1,2048]{1,0:T(1,128)}, f32[1,2048]{1,0:T(1,128)S(1)}, u32[]{:S(2)}) copy-start(f32[1,2048]{1,0:T(1,128)S(1)} %get-tuple-element.29) | copy-start | bytes 24580
  13.7 81.3 %copy-start.10 = (f32[1,2048]{1,0:T(1,128)}, f32[1,2048]{1,0:T(1,128)S(1)}, u32[]{:S(2)}) copy-start(f32[1,2048]{1,0:T(1,128)S(1)} %get-tuple-element.30) | copy-start | bytes 24580
  13.7 81.3 %copy-start.11 = (f32[1,2048]{1,0:T(1,128)}, f32[1,2048]{1,0:T(1,128)S(1)}, u32[]{:S(2)}) copy-start(f32[1,2048]{1,0:T(1,128)S(1)} %get-tuple-element.31) | copy-start | bytes 24580
  13.7 81.3 %copy-start.12 = (f32[1,2048]{1,0:T(1,128)}, f32[1,2048]{1,0:T(1,128)S(1)}, u32[]{:S(2)}) copy-start(f32[1,2048]{1,0:T(1,128)S(1)} %get-tuple-element.32) | copy-start | bytes 24580
  13.7 81.3 %copy-start.13 = (f32[1,2048]{1,0:T(1,128)}, f32[1,2048]{1,0:T(1,128)S(1)}, u32[]{:S(2)}) copy-start(f32[1,2048]{1,0:T(1,128)S(1)} %get-tuple-element.33) | copy-start | bytes 24580
  86.2 8.9 %copy-start.4 = (s32[1280]{0:T(1024)S(1)}, s32[1280]{0:T(1024)}, u32[]{:S(2)}) copy-start(s32[1280]{0:T(1024)} %param.17) | copy-start | bytes 15364
  86.2 9.3 %copy-start.16 = (s32[1280]{0:T(1024)S(1)}, s32[1280]{0:T(1024)}, u32[]{:S(2)}) copy-start(s32[1280]{0:T(1024)} %param.18) | copy-start | bytes 15364
  86.2 9.3 %copy-start.17 = (f32[3]{0:T(128)S(1)}, f32[3]{0:T(128)}, u32[]{:S(2)}) copy-start(f32[3]{0:T(128)} %param.15) | copy-start | bytes 40
  95.1 75.5 %copy-start.15 = (f32[64]{0:T(128)S(1)}, f32[64]{0:T(128)}, u32[]{:S(2)}) copy-start(f32[64]{0:T(128)} %param.16) | copy-start | bytes 772
  95.1 170.4 %all-reduce.14.cloned.1.call-start = ((), (), s32[]{:S(2)}) async-start(), calls=%async_computation.2 | async-start | bytes 1048576 | tf_op jit(solution)/shard_map/psum | solution.py:109
  169.9 0.7 copy-start.2
  182.7 8.7 %copy-start.1 = (bf16[1024,2048]{1,0:T(8,128)(2,1)S(1)}, bf16[1024,2048]{1,0:T(8,128)(2,1)}, u32[]{:S(2)}) copy-start(bf16[1024,2048]{1,0:T(8,128)(2,1)} %param.11) | copy-start | bytes 12582916
Sparse Core Ops, SparseCore 0:
  10.8 75.4 all-reduce.9
  95.2 70.5 all-reduce.11
  193.2 72.2 all-reduce.13
where the time goes:
time: 280 us; the launch traced here: 279 us
  waiting for transfers between devices  215 us (77%)
  matrix products  35 us (12%)
  between operations  13.6 us (5%)
  blocking collectives  11.1 us (4%)
  local copies, waits for them, and re-layouts  3.06 us (1%)
    psum x1, waiting for transfers between devices, shards(): lax.psum(jnp.dot(beta_vectors.T, band_coeffs, preferred_element_type=jnp....  72.5 us
    psum x1, waiting for transfers between devices, shards(): lax.psum(jnp.dot(beta_vectors.T, wave_half, preferred_element_type=jnp.fl...  72.4 us
    psum x1, waiting for transfers between devices, shards(): summed = lax.psum(partial_value, 'ga')  69.8 us
    psum x1, blocking collectives, shards(): lax.psum(occupancy(extended, band_weight, mask, ORB_REACH, norbit), 'band')  11.1 us
    dot_general x1, matrix products, shards(): jnp.dot(atomic_waves.T, correlation_psi, preferred_element_type=jnp.float32)  8.77 us
    dot_general x1, matrix products, shards(): jnp.dot(beta_vectors, correction, preferred_element_type=jnp.float32)  7.46 us
    dot_general x1, matrix products, shards(): rotated = jnp.dot(ortho_full, mixed, precision=highest)  5.79 us
  transfers between devices with their start and end apart: 3, of which 3 were waited for; matrix products, arithmetic and copies ran while one was open for 1% of the time, Pallas kernels for 0%

commit v1 on v0

--- a/solution.py
+++ b/solution.py
@@ -82,9 +82,8 @@
     nbeta = beta_vectors.shape[1]
     norbit = atomic_waves.shape[1]
     coupling = beta_matrix(beta_coupling, beta_start)
-    beta_correlation = lax.psum(
-        jnp.dot(beta_vectors.T, band_coeffs, preferred_element_type=jnp.float32), "ga"
-    )
+    q_in = jnp.dot(beta_vectors.T, band_coeffs, preferred_element_type=jnp.float32)
+    beta_correlation = jnp.sum(jax.lax.all_gather(q_in, axis_name="ga"), 0)
     corrected = band_apply(
         coupling, jnp.pad(beta_correlation, ((BETA_REACH, BETA_REACH), (0, 0))), BETA_REACH, nbeta
     ).astype(jnp.bfloat16)

time: 280 us -> 285 us (1.018)
  local copies, waits for them, and re-layouts: 3.06 us -> 7.63 us
    all_gather x0 -> x1, waiting for transfers between devices: none -> 72.5 us  [shards(): beta_correlation = jnp.sum(jax.lax.all_gather(q_in, axis_name='ga'), 0)]
    psum x1 -> x0, waiting for transfers between devices: 72.5 us -> none  [shards(): lax.psum(jnp.dot(beta_vectors.T, band_coeffs, preferred_element_type=jnp....]
    unnamed x36 -> x39, local copies, waits for them, and re-layouts: 0.78 us -> 5.35 us
where the time goes in v1:
time: 285 us
  waiting for transfers between devices  214 us (75%)
  matrix products  34.8 us (12%)
  between operations  13.6 us (5%)
  blocking collectives  11.1 us (4%)
  local copies, waits for them, and re-layouts  7.63 us (3%)
  other arithmetic  3.78 us (1%)
    all_gather x1, waiting for transfers between devices, shards(): beta_correlation = jnp.sum(jax.lax.all_gather(q_in, axis_name='ga'), 0)  72.5 us
    psum x1, waiting for transfers between devices, shards(): lax.psum(jnp.dot(beta_vectors.T, wave_half, preferred_element_type=jnp.fl...  72.4 us
    psum x1, waiting for transfers between devices, shards(): summed = lax.psum(partial_value, 'ga')  69.2 us
    psum x1, blocking collectives, shards(): lax.psum(occupancy(extended, band_weight, mask, ORB_REACH, norbit), 'band')  11.1 us
    dot_general x1, matrix products, shards(): jnp.dot(atomic_waves.T, correlation_psi, preferred_element_type=jnp.float32)  8.63 us
    dot_general x1, matrix products, shards(): jnp.dot(beta_vectors, correction, preferred_element_type=jnp.float32)  7.41 us
    dot_general x1, matrix products, shards(): rotated = jnp.dot(ortho_full, mixed, precision=highest)  5.79 us
  transfers between devices with their start and end apart: 3, of which 3 were waited for; matrix products, arithmetic and copies ran while one was open for 1% of the time, Pallas kernels for 0%

profile of v1, /device:TPU:0, one launch (start us, length us, event | category | flops | bytes accessed | tf_op | source)
XLA Modules:
  0.0 285.1 jit_solution(8973181449006062445)
XLA Ops:
  6.5 4.0 %fusion.134 = f32[2048,64]{0,1:T(8,128)} fusion(bf16[1024,64]{0,1:T(8,128)(2,1)} %param.10, bf16[1024,2048]{1,0:T(8,128)(2,1)} %param.11), kind=kOutput, calls=%fused_computation.208 | convolution fusion | flops 268435456 | bytes 4849664 | tf_op jit(solution)/shard_map/dot_general | solution.py:85
  10.6 0.0 all-gather.3.cloned.1.call-update
  10.6 0.0 all-reduce.9.cloned.1.call-start
  10.7 0.1 multiply_bitcast_fusion.8
  10.8 0.2 multiply_bitcast_fusion
  11.0 0.2 stack.160
  11.2 0.7 fusion.117
  11.9 1.7 stack.181
  13.6 0.1 fusion.132
  13.7 72.5 %all-gather.3.cloned.1.call-done = f32[16384,64]{0,1:T(8,128)} async-done(((f32[2048,64]{0,1:T(8,128)}), f32[16384,64]{0,1:T(8,128)}) %all-gather.3.cloned.1.call-update) | async-done | bytes 4194320 | tf_op jit(solution)/shard_map/all_gather | solution.py:86
  86.3 4.6 %copy.11 = f32[8,8,8,2048]{3,2,1,0:T(8,128)S(1)} copy(f32[8,8,8,2048]{3,1,2,0:T(8,128)} %bitcast.78) | data formatting | bytes 8388608
  90.8 1.8 bitcast_reduce_fusion
  92.7 8.6 %convolution_bitcast_fusion.2 = f32[1280,64]{0,1:T(8,128)} fusion(bf16[1024,1280]{1,0:T(8,128)(2,1)} %param.12, bf16[1024,2048]{1,0:T(8,128)(2,1)} %param.11, f32[2048,64]{0,1:T(8,128)} %bitcast_reduce_fusion, f32[2048]{0:T(1024)S(1)} %bitcast.91, f32[2048]{0:T(1024)S(1)} %bitcast.93, f32[2048]{0:T(1024)S(1)} %bitcast.95, f32[2048]{0:T(1024)S(1)} %bitcast.97, ...), kind=kOutput, calls=%fused_computation.3 | convolution fusion | flops 439287808 | bytes 7888896 | tf_op jit(solution)/shard_map/dot_general | solution.py:94
  101.4 0.0 all-reduce.9.cloned.1.call-update
  101.4 0.0 all-reduce.11.cloned.1.call-start
  101.4 0.1 fusion.116
  101.7 0.1 stack.208
  101.8 0.5 convolution_reduce_fusion
  102.3 69.2 %all-reduce.9.cloned.1.call-done = f32[1280,64]{0,1:T(8,128)} async-done(((f32[1280,64]{0,1:T(8,128)}), f32[1280,64]{0,1:T(8,128)}) %all-reduce.9.cloned.1.call-update) | async-done | bytes 327696 | tf_op jit(solution)/shard_map/psum | solution.py:98
  171.5 4.0 %convolution_bitcast_fusion.1 = f32[1280,64]{0,1:T(8,128)S(1)} fusion(f32[1280,64]{0,1:T(8,128)} %all-reduce.9.cloned.1.call-done, bf16[1280,1280]{1,0:T(8,128)(2,1)S(1)} %copy-done), kind=kOutput, calls=%fused_computation.2 | convolution fusion | flops 1258291200 | bytes 3932160 | tf_op jit(solution)/shard_map/dot_general | solution.py:99
  175.6 0.7 copy-done.2
  176.3 0.8 fusion.26
  177.2 0.1 stack.191
  177.3 11.1 %psum.22 = f32[9,1280]{1,0:T(8,128)S(1)} all-reduce(f32[9,1280]{1,0:T(8,128)S(1)} %mul.535), channel_id=1, replica_groups=mesh['ga'=8,'band'=4] {'band'}, use_global_device_ids=true, to_apply=%region_11.12 | all-reduce | flops 11520 | bytes 92160 | tf_op jit(solution)/shard_map/psum | solution.py:102
  188.4 0.1 multiply_multiply_fusion.9
  188.5 0.1 slice_reduce_fusion.8
  188.6 5.8 %convolution_convert_fusion = bf16[64,1280]{1,0:T(8,128)(2,1)S(1)} fusion(bf16[1280,1280]{1,0:T(8,128)(2,1)S(1)} %copy-done, f32[1280,64]{0,1:T(8,128)} %copy-done.2, f32[1280]{0:T(1024)S(1)} %get-tuple-element.15, f32[1280]{0:T(1024)S(1)} %get-tuple-element.16, f32[1280]{0:T(1024)S(1)} %get-tuple-element.17, f32[1280]{0:T(1024)S(1)} %get-tuple-element.18, ...), kind=kOutput, calls=%fused_computation.4 | convolution fusion | flops 1259765760 | bytes 3814400 | tf_op jit(solution)/shard_map/dot_general | solution.py:104
  194.4 2.6 fusion.133
  197.0 1.7 convolution_bitcast_fusion
  198.7 0.0 all-reduce.11.cloned.1.call-update
  198.7 72.4 %all-reduce.11.cloned.1.call-done = f32[2048,64]{0,1:T(8,128)} async-done(((f32[2048,64]{0,1:T(8,128)}), f32[2048,64]{0,1:T(8,128)}) %all-reduce.11.cloned.1.call-update) | async-done | bytes 524304 | tf_op jit(solution)/shard_map/psum | solution.py:108
  271.1 7.4 %fusion.3 = bf16[1024,64]{0,1:T(8,128)(2,1)} fusion(f32[64,1024]{1,0:T(8,128)S(1)} %fusion.133, bf16[1024,2048]{1,0:T(8,128)(2,1)} %param.11, f32[2048,64]{0,1:T(8,128)} %all-reduce.11.cloned.1.call-done, f32[2048]{0:T(1024)S(1)} %bitcast.92, f32[2048]{0:T(1024)} %bitcast.94, f32[2048]{0:T(1024)} %bitcast.96, f32[2048]{0:T(1024)} %bitcast.98, ...), kind=kOutput, calls=%fused_computation.10 | convolution fusion | flops 271450112 | bytes 5201920 | tf_op jit(solution)/shard_map/dot_general | solution.py:115
  (60 shorter events, 0.2 us)
Async XLA Ops:
  6.5 165.0 %copy-start = (bf16[1280,1280]{1,0:T(8,128)(2,1)S(1)}, bf16[1280,1280]{1,0:T(8,128)(2,1)}, u32[]{:S(2)}) copy-start(bf16[1280,1280]{1,0:T(8,128)(2,1)} %param.14) | copy-start | bytes 9830404
  6.5 4.1 %copy-start.3 = (f32[2048,11]{0,1:T(8,128)S(1)}, f32[2048,11]{0,1:T(8,128)}, u32[]{:S(2)}) copy-start(f32[2048,11]{0,1:T(8,128)} %param.13) | copy-start | bytes 270340
  6.5 4.6 %copy-start.15 = (s32[2048]{0:T(1024)S(1)}, s32[2048]{0:T(1024)}, u32[]{:S(2)}) copy-start(s32[2048]{0:T(1024)} %param.19) | copy-start | bytes 24580
  6.5 79.7 %all-gather.3.cloned.1.call-start = ((), (), s32[]{:S(2)}) async-start(), calls=%async_computation.2 | async-start | bytes 4718592 | tf_op jit(solution)/shard_map/all_gather | solution.py:86
  10.6 160.9 %all-reduce.9.cloned.1.call-start = ((), (), s32[]{:S(2)}) async-start(), calls=%async_computation | async-start | bytes 655360 | tf_op jit(solution)/shard_map/psum | solution.py:98
  13.6 79.0 %copy-start.6 = (f32[1,2048]{1,0:T(1,128)}, f32[1,2048]{1,0:T(1,128)S(1)}, u32[]{:S(2)}) copy-start(f32[1,2048]{1,0:T(1,128)S(1)} %get-tuple-element.25) | copy-start | bytes 24580
  13.6 79.0 %copy-start.7 = (f32[1,2048]{1,0:T(1,128)}, f32[1,2048]{1,0:T(1,128)S(1)}, u32[]{:S(2)}) copy-start(f32[1,2048]{1,0:T(1,128)S(1)} %get-tuple-element.26) | copy-start | bytes 24580
  13.7 79.0 %copy-start.8 = (f32[1,2048]{1,0:T(1,128)}, f32[1,2048]{1,0:T(1,128)S(1)}, u32[]{:S(2)}) copy-start(f32[1,2048]{1,0:T(1,128)S(1)} %get-tuple-element.27) | copy-start | bytes 24580
  13.7 79.0 %copy-start.9 = (f32[1,2048]{1,0:T(1,128)}, f32[1,2048]{1,0:T(1,128)S(1)}, u32[]{:S(2)}) copy-start(f32[1,2048]{1,0:T(1,128)S(1)} %get-tuple-element.28) | copy-start | bytes 24580
  13.7 79.0 %copy-start.10 = (f32[1,2048]{1,0:T(1,128)}, f32[1,2048]{1,0:T(1,128)S(1)}, u32[]{:S(2)}) copy-start(f32[1,2048]{1,0:T(1,128)S(1)} %get-tuple-element.29) | copy-start | bytes 24580
  13.7 79.0 %copy-start.11 = (f32[1,2048]{1,0:T(1,128)}, f32[1,2048]{1,0:T(1,128)S(1)}, u32[]{:S(2)}) copy-start(f32[1,2048]{1,0:T(1,128)S(1)} %get-tuple-element.30) | copy-start | bytes 24580
  13.7 79.0 %copy-start.12 = (f32[1,2048]{1,0:T(1,128)}, f32[1,2048]{1,0:T(1,128)S(1)}, u32[]{:S(2)}) copy-start(f32[1,2048]{1,0:T(1,128)S(1)} %get-tuple-element.31) | copy-start | bytes 24580
  13.7 79.0 %copy-start.13 = (f32[1,2048]{1,0:T(1,128)}, f32[1,2048]{1,0:T(1,128)S(1)}, u32[]{:S(2)}) copy-start(f32[1,2048]{1,0:T(1,128)S(1)} %get-tuple-element.32) | copy-start | bytes 24580
  13.7 79.0 %copy-start.14 = (f32[1,2048]{1,0:T(1,128)}, f32[1,2048]{1,0:T(1,128)S(1)}, u32[]{:S(2)}) copy-start(f32[1,2048]{1,0:T(1,128)S(1)} %get-tuple-element.33) | copy-start | bytes 24580
  90.8 1.9 copy-start.4
  92.7 8.7 %copy-start.5 = (s32[1280]{0:T(1024)S(1)}, s32[1280]{0:T(1024)}, u32[]{:S(2)}) copy-start(s32[1280]{0:T(1024)} %param.17) | copy-start | bytes 15364
  92.7 9.0 %copy-start.17 = (s32[1280]{0:T(1024)S(1)}, s32[1280]{0:T(1024)}, u32[]{:S(2)}) copy-start(s32[1280]{0:T(1024)} %param.18) | copy-start | bytes 15364
  92.7 9.0 %copy-start.18 = (f32[3]{0:T(128)S(1)}, f32[3]{0:T(128)}, u32[]{:S(2)}) copy-start(f32[3]{0:T(128)} %param.15) | copy-start | bytes 40
  101.4 74.9 %copy-start.16 = (f32[64]{0:T(128)S(1)}, f32[64]{0:T(128)}, u32[]{:S(2)}) copy-start(f32[64]{0:T(128)} %param.16) | copy-start | bytes 772
  101.4 169.7 %all-reduce.11.cloned.1.call-start = ((), (), s32[]{:S(2)}) async-start(), calls=%async_computation.1 | async-start | bytes 1048576 | tf_op jit(solution)/shard_map/psum | solution.py:108
  175.5 0.7 copy-start.2
  188.4 8.7 %copy-start.1 = (bf16[1024,2048]{1,0:T(8,128)(2,1)S(1)}, bf16[1024,2048]{1,0:T(8,128)(2,1)}, u32[]{:S(2)}) copy-start(bf16[1024,2048]{1,0:T(8,128)(2,1)} %param.11) | copy-start | bytes 12582916
Sparse Core Ops, SparseCore 0:
  10.7 75.4 all-gather.2
  101.5 69.9 all-reduce.8
  198.8 72.2 all-reduce.10
